TPU v7x, 512 devices: a whole 4x8x8 slice. The times are simulated.
512 devices in a mesh: lon: 8 (over y_lo, core), lat: 64 (over x, y_hi, z).
Axes of the slice: x: 4, y: 8 (y_hi: 2, y_lo: 4; y = y_hi * 4 + y_lo), z: 8, core: 2. Of those that a mesh axis runs over, the one named last changes fastest.
Arguments:
- ocean_state: bfloat16 [1, 384, 512, 256], P(None, 'lat', 'lon'), may hold values from -6 to 6
- land_sea: int32 [1, 384, 512], P(None, 'lat', 'lon'), may hold values 0 or 1
- cotangent: bfloat16 [1, 384, 512, 256], P(None, 'lat', 'lon'), may hold values from -6 to 6
- dw_kernel: float32 [7, 7, 256], replicated, may hold values from -0.875 to 0.875
- dw_bias: float32 [256], replicated, may hold values from -3 to 3
- ln_gain: float32 [256], replicated, may hold values from 0.1 to 1.9
- ln_bias: float32 [256], replicated, may hold values from -2 to 2
- w_in: bfloat16 [256, 1024], replicated, may hold values from -0.375 to 0.375
- b_in: float32 [1024], replicated, may hold values from -2 to 2
- w_out: bfloat16 [1024, 256], replicated, may hold values from -0.1875 to 0.1875
- b_out: float32 [256], replicated, may hold values from -2 to 2
- layer_scale: float32 [256], replicated, may hold values from 0.3 to 1.5
Outputs:
- output: bfloat16 [1, 384, 512, 256], P(None, 'lat', 'lon')
- grad_state: bfloat16 [1, 384, 512, 256], P(None, 'lat', 'lon')
- grad_kernel: float32 [7, 7, 256], replicated
- grad_dw_bias: float32 [256], replicated
- grad_ln_gain: float32 [256], replicated
- grad_ln_bias: float32 [256], replicated
- grad_w_in: float32 [256, 1024], replicated
- grad_b_in: float32 [1024], replicated
- grad_w_out: float32 [1024, 256], replicated
- grad_b_out: float32 [256], replicated
- grad_scale: float32 [256], replicated
All inputs are finite; a program needn't handle non-finite values. No bound on the sum of `land_sea` on one device may be relied on, other than what follows from the above.
Results may differ from a plain program's by a relative error of at most 0.0085.
Values may be sent and summed in bfloat16 or wider, within the bound.
No kernel may reach another device: no remote copies, remote signals or barrier semaphores. Data moves between devices by JAX's collectives and lax.ppermute only.
A program may use at most 64 MiB of HBM per device.

v0:
```python
import jax
import jax.numpy as jnp
from jax import lax
from jax.sharding import PartitionSpec as P


def extended(array, sides, width, wrap):
    for axis, dim in sides:
        size, length = (lax.axis_size(axis), array.shape[dim])
        up = [(i, (i + 1) % size) for i in range(size if wrap else size - 1)]
        down = [(j, i) for i, j in up]
        last = lax.slice_in_dim(array, length - width, length, axis=dim)
        leading = lax.slice_in_dim(array, 0, width, axis=dim)
        before = lax.ppermute(last, axis, up)
        after = lax.ppermute(leading, axis, down)
        array = jnp.concatenate([before, array, after], axis=dim)
    return array


def depthwise(padded, kernel, num_rows, num_cols):
    summed = jnp.zeros((padded.shape[0], num_rows, num_cols, padded.shape[3]), jnp.float32)
    for row_off in range(7):
        for col_off in range(7):
            summed = (
                summed
                + padded[:, row_off : row_off + num_rows, col_off : col_off + num_cols, :].astype(
                    jnp.float32
                )
                * kernel[row_off, col_off]
            )
    return summed


def transposed(padded, kernel, num_rows, num_cols):
    summed = jnp.zeros((padded.shape[0], num_rows, num_cols, padded.shape[3]), jnp.float32)
    for row_off in range(7):
        for col_off in range(7):
            summed = (
                summed
                + padded[
                    :, 6 - row_off : 6 - row_off + num_rows, 6 - col_off : 6 - col_off + num_cols, :
                ].astype(jnp.float32)
                * kernel[row_off, col_off]
            )
    return summed


def kernel_terms(padded, grad_depth, num_rows, num_cols):
    grad_float = grad_depth.astype(jnp.float32)
    rows_out = []
    for row_off in range(7):
        cols_out = []
        for col_off in range(7):
            window = padded[
                :, row_off : row_off + num_rows, col_off : col_off + num_cols, :
            ].astype(jnp.float32)
            cols_out.append(jnp.sum(window * grad_float, axis=(0, 1, 2)))
        rows_out.append(jnp.stack(cols_out))
    return jnp.stack(rows_out)


def forward_tokens(depth_out, ln_gain, ln_bias, w_in, b_in, w_out, b_out):
    center = depth_out - jnp.mean(depth_out, axis=-1, keepdims=True)
    inv_std = lax.rsqrt(jnp.mean(center * center, axis=-1, keepdims=True) + 1e-06)
    norm_hat = center * inv_std
    normed = (norm_hat * ln_gain + ln_bias).astype(jnp.bfloat16)
    pre_act = jnp.dot(normed, w_in, preferred_element_type=jnp.float32) + b_in
    activated = jax.nn.gelu(pre_act, approximate=True).astype(jnp.bfloat16)
    branch = jnp.dot(activated, w_out, preferred_element_type=jnp.float32) + b_out
    return (norm_hat, inv_std, normed, pre_act, activated, branch)


def backward_tokens(masked, norm_hat, inv_std, pre_act, ln_gain, w_in, w_out, layer_scale):
    grad_branch = (masked * layer_scale).astype(jnp.bfloat16)
    grad_act = lax.dot_general(
        grad_branch, w_out, (((1,), (1,)), ((), ())), preferred_element_type=jnp.float32
    )
    unused, pull_back = jax.vjp(lambda v: jax.nn.gelu(v, approximate=True), pre_act)
    grad_pre = pull_back(grad_act)[0].astype(jnp.bfloat16)
    grad_norm = lax.dot_general(
        grad_pre, w_in, (((1,), (1,)), ((), ())), preferred_element_type=jnp.float32
    )
    scaled = grad_norm * ln_gain
    grad_depth = (
        inv_std
        * (
            scaled
            - jnp.mean(scaled, axis=-1, keepdims=True)
            - norm_hat * jnp.mean(scaled * norm_hat, axis=-1, keepdims=True)
        )
    ).astype(jnp.bfloat16)
    return (grad_branch, grad_pre, grad_norm, grad_depth)


def weight_terms(masked, branch, grad_branch, activated, normed, grad_pre, grad_norm, norm_hat):
    dims = (((0,), (0,)), ((), ()))
    grad_w_in = lax.dot_general(normed, grad_pre, dims, preferred_element_type=jnp.float32)
    grad_w_out = lax.dot_general(activated, grad_branch, dims, preferred_element_type=jnp.float32)
    return (
        grad_w_in,
        grad_w_out,
        jnp.sum(grad_pre.astype(jnp.float32), axis=0),
        jnp.sum(grad_branch.astype(jnp.float32), axis=0),
        jnp.sum(masked * branch, axis=0),
        jnp.sum(grad_norm * norm_hat, axis=0),
        jnp.sum(grad_norm, axis=0),
    )


def local(
    ocean_state,
    land_sea,
    cotangent,
    dw_kernel,
    dw_bias,
    ln_gain,
    ln_bias,
    w_in,
    b_in,
    w_out,
    b_out,
    layer_scale,
):
    num_batch, num_rows, num_cols, channels = ocean_state.shape
    mask_float = land_sea.astype(jnp.float32)[..., None]
    lon_ext = extended(ocean_state, (("lon", 2),), 3, True)
    padded = extended(lon_ext, (("lat", 1),), 3, False)
    depth_out = depthwise(padded, dw_kernel, num_rows, num_cols) + dw_bias
    masked = (mask_float * cotangent.astype(jnp.float32)).reshape(-1, channels)
    norm_hat, inv_std, normed, pre_act, activated, branch = forward_tokens(
        depth_out.reshape(-1, channels), ln_gain, ln_bias, w_in, b_in, w_out, b_out
    )
    grad_branch, grad_pre, grad_norm, grad_flat = backward_tokens(
        masked, norm_hat, inv_std, pre_act, ln_gain, w_in, w_out, layer_scale
    )
    grad_terms = weight_terms(
        masked, branch, grad_branch, activated, normed, grad_pre, grad_norm, norm_hat
    )
    grad_depth = grad_flat.reshape(num_batch, num_rows, num_cols, channels)
    grad_ext = extended(grad_depth, (("lon", 2),), 3, True)
    grad_pad = extended(grad_ext, (("lat", 1),), 3, False)
    branch_own = branch.reshape(num_batch, num_rows, num_cols, channels)
    output = (ocean_state.astype(jnp.float32) + mask_float * layer_scale * branch_own).astype(
        jnp.bfloat16
    )
    grad_state = (
        cotangent.astype(jnp.float32) + transposed(grad_pad, dw_kernel, num_rows, num_cols)
    ).astype(jnp.bfloat16)
    kernel_part = kernel_terms(padded, grad_depth, num_rows, num_cols)
    bias_part = jnp.sum(grad_depth.astype(jnp.float32), axis=(0, 1, 2))
    grad_w_in, grad_w_out, grad_b_in, grad_b_out, grad_scale, grad_ln_gain, grad_ln_bias = (
        grad_terms
    )
    reduced = lax.psum(
        (
            grad_w_in,
            grad_w_out,
            grad_b_in,
            grad_b_out,
            grad_scale,
            grad_ln_gain,
            grad_ln_bias,
            kernel_part,
            bias_part,
        ),
        ("lon", "lat"),
    )
    (
        grad_w_in,
        grad_w_out,
        grad_b_in,
        grad_b_out,
        grad_scale,
        grad_ln_gain,
        grad_ln_bias,
        kernel_part,
        bias_part,
    ) = reduced
    all_cells = num_batch * num_rows * num_cols * lax.axis_size("lon") * lax.axis_size("lat")
    factor = 1.0 / jnp.sqrt(jnp.float32(all_cells))
    return (
        output,
        grad_state,
        kernel_part * factor,
        bias_part * factor,
        grad_ln_gain * factor,
        grad_ln_bias * factor,
        grad_w_in * factor,
        grad_b_in * factor,
        grad_w_out * factor,
        grad_b_out * factor,
        grad_scale * factor,
    )


def solution(mesh):
    in_specs = (
        P(None, "lat", "lon", None),
        P(None, "lat", "lon"),
        P(None, "lat", "lon", None),
        P(),
        P(),
        P(),
        P(),
        P(),
        P(),
        P(),
        P(),
        P(),
    )
    out_specs = (
        P(None, "lat", "lon", None),
        P(None, "lat", "lon", None),
        P(),
        P(),
        P(),
        P(),
        P(),
        P(),
        P(),
        P(),
        P(),
    )
    return jax.shard_map(local, mesh=mesh, in_specs=in_specs, out_specs=out_specs, check_vma=False)
```

profile of v0, /device:TPU:1, one launch (start us, length us, event | category | flops | bytes accessed | tf_op | source)
XLA Modules:
  0.0 450.9 jit_solution(3544239886626899903)
XLA Ops:
  7.3 0.8 fusion.147
  8.1 8.8 %collective-permute-start.1 = (bf16[1,6,3,256]{3,2,1,0:T(4,128)(2,1)S(1)}, bf16[1,6,3,256]{3,2,1,0:T(4,128)(2,1)S(1)}, u32[]{:S(2)}, u32[]{:S(2)}) collective-permute-start(bf16[1,6,3,256]{3,2,1,0:T(4,128)(2,1)S(1)} %get-tuple-element.102), channel_id=1, source_target_pairs={{64,0},{128,64},{192,128},{256,192},{320,256},{384,320},{448,384},... | collective-permute-start | bytes 27656 | tf_op jit(solution)/shard_map/ppermute | solution.py:15
  16.9 1.9 collective-permute-start
  18.8 0.9 fusion.150
  19.8 1.0 fusion.148
  20.8 1.0 fusion.149
  21.8 0.9 constant_dynamic-update-slice_fusion.1
  22.7 0.7 convert_element_type.400
  23.4 1.0 pad_maximum_fusion.2
  24.5 1.3 collective-permute-start.2
  25.8 1.3 collective-permute-start.3
  27.5 3.8 collective-permute-done.3
  31.4 3.2 fusion.142
  35.7 0.6 convolution_add_fusion.1
  36.6 0.9 convert_reduce_fusion.1
  37.6 1.3 convert_reduce_fusion
  39.7 0.8 fusion.102
  40.5 0.8 fusion.130
  41.2 1.4 fusion.151
  42.7 1.7 fusion.141
  44.4 3.6 collective-permute-start.4
  48.0 2.6 collective-permute-start.5
  50.6 0.7 fusion.129
  51.6 111.9 %all-reduce = (f32[7,7,256]{2,1,0:T(8,128)S(1)}, f32[256]{0:T(256)S(1)}, f32[256]{0:T(256)S(1)}, f32[256]{0:T(256)S(1)}, f32[1024]{0:T(1024)S(1)}, /*index=5*/f32[256]{0:T(256)S(1)}, f32[256]{0:T(256)S(1)}) all-reduce(f32[7,7,256]{2,1,0:T(8,128)S(1)} %constant_dynamic-update-slice_fusion.2, ...), channel_id=1, replica_groups=mesh['lon'=8,'lat'=64] {'lon','lat'}, use_global_device_ids=true, to_apply=%region_53.0 | all-reduce | flops 14848 | bytes 118784 | tf_op jit(solution)/shard_map/psum | solution.py:154
  163.5 0.6 broadcast_multiply_fusion.2
  167.1 1.3 collective-permute-start.6
  168.4 4.0 collective-permute-start.7
  173.0 1.2 collective-permute-done.7
  174.3 3.8 fusion.55
  178.0 262.5 %all-reduce.4.cloned.1.call-done = (f32[256,1024]{1,0:T(8,128)}, f32[1024,256]{1,0:T(8,128)}) async-done(((f32[256,1024]{1,0:T(8,128)}, f32[1024,256]{1,0:T(8,128)}), (f32[256,1024]{1,0:T(8,128)}, f32[1024,256]{1,0:T(8,128)})) %all-reduce.4.cloned.1.call-update) | async-done | bytes 2097168 | tf_op jit(solution)/shard_map/psum | solution.py:154
  440.5 2.4 broadcast_multiply_fusion.1
  443.0 1.1 broadcast_multiply_fusion
  (69 shorter events, 6.7 us)
Async XLA Ops:
  7.2 28.0 %copy-start = (bf16[256,1024]{1,0:T(8,128)(2,1)S(1)}, bf16[256,1024]{1,0:T(8,128)(2,1)}, u32[]{:S(2)}) copy-start(bf16[256,1024]{1,0:T(8,128)(2,1)} %param.19) | copy-start | bytes 1572868
  7.2 24.1 %copy-start.1 = (bf16[1,6,64,256]{3,2,1,0:T(8,128)(2,1)S(1)}, bf16[1,6,64,256]{3,2,1,0:T(8,128)(2,1)}, u32[]{:S(2)}) copy-start(bf16[1,6,64,256]{3,2,1,0:T(8,128)(2,1)} %param.12) | copy-start | bytes 589828
  7.2 24.1 %copy-start.8 = (f32[256]{0:T(256)S(1)}, f32[256]{0:T(256)}, u32[]{:S(2)}) copy-start(f32[256]{0:T(256)} %param.16) | copy-start | bytes 3076
  7.2 433.3 %all-reduce.4.cloned.1.call-start = ((), (), s32[]{:S(2)}) async-start(), calls=%async_computation | async-start | bytes 4194304 | tf_op jit(solution)/shard_map/psum | solution.py:154
  8.1 15.3 %collective-permute-start.1 = (bf16[1,6,3,256]{3,2,1,0:T(4,128)(2,1)S(1)}, bf16[1,6,3,256]{3,2,1,0:T(4,128)(2,1)S(1)}, u32[]{:S(2)}, u32[]{:S(2)}) collective-permute-start(bf16[1,6,3,256]{3,2,1,0:T(4,128)(2,1)S(1)} %get-tuple-element.102), channel_id=1, source_target_pairs={{64,0},{128,64},{192,128},{256,192},{320,256},{384,320},{448,384},... | collective-permute-start | bytes 27656 | tf_op jit(solution)/shard_map/ppermute | solution.py:15
  16.9 6.5 %collective-permute-start = (bf16[1,6,3,256]{3,2,1,0:T(4,128)(2,1)S(1)}, bf16[1,6,3,256]{3,2,1,0:T(4,128)(2,1)S(1)}, u32[]{:S(2)}, u32[]{:S(2)}) collective-permute-start(bf16[1,6,3,256]{3,2,1,0:T(4,128)(2,1)S(1)} %get-tuple-element.101), channel_id=1, source_target_pairs={{0,64},{64,128},{128,192},{192,256},{256,320},{320,384},{384,448},... | collective-permute-start | bytes 27656 | tf_op jit(solution)/shard_map/ppermute | solution.py:14
  24.5 3.0 collective-permute-start.2
  25.8 5.5 %collective-permute-start.3 = (bf16[1,3,70,256]{3,2,1,0:T(8,128)(2,1)S(1)}, bf16[1,3,70,256]{3,2,1,0:T(8,128)(2,1)S(1)}, u32[]{:S(2)}, u32[]{:S(2)}) collective-permute-start(bf16[1,3,70,256]{3,2,1,0:T(8,128)(2,1)S(1)} %get-tuple-element.96), channel_id=1, source_target_pairs={{1,0},{2,1},{3,2},{4,3},{5,4},{6,5},{7,6},{8,7},{9,8},{10,9},{11,1... | collective-permute-start | bytes 322568 | tf_op jit(solution)/shard_map/ppermute | solution.py:15
  31.4 3.6 copy-start.5
  31.4 3.6 copy-start.7
  31.4 3.8 copy-start.4
  34.6 1.0 copy-start.9
  34.6 1.0 copy-start.10
  35.7 0.9 copy-start.3
  35.7 0.9 copy-start.6
  44.4 122.7 %collective-permute-start.4 = (bf16[1,6,3,256]{3,2,1,0:T(4,128)(2,1)S(1)}, bf16[1,6,3,256]{3,2,1,0:T(4,128)(2,1)S(1)}, u32[]{:S(2)}, u32[]{:S(2)}) collective-permute-start(bf16[1,6,3,256]{3,2,1,0:T(4,128)(2,1)S(1)} %get-tuple-element.100), channel_id=1, source_target_pairs={{0,64},{64,128},{128,192},{192,256},{256,320},{320,384},{384,448},... | collective-permute-start | bytes 27656 | tf_op jit(solution)/shard_map/ppermute | solution.py:14
  48.0 119.0 %collective-permute-start.5 = (bf16[1,6,3,256]{3,2,1,0:T(4,128)(2,1)S(1)}, bf16[1,6,3,256]{3,2,1,0:T(4,128)(2,1)S(1)}, u32[]{:S(2)}, u32[]{:S(2)}) collective-permute-start(bf16[1,6,3,256]{3,2,1,0:T(4,128)(2,1)S(1)} %get-tuple-element.99), channel_id=1, source_target_pairs={{64,0},{128,64},{192,128},{256,192},{320,256},{384,320},{448,384},... | collective-permute-start | bytes 27656 | tf_op jit(solution)/shard_map/ppermute | solution.py:15
  167.1 5.9 %collective-permute-start.6 = (bf16[1,3,70,256]{3,2,1,0:T(8,128)(2,1)S(1)}, bf16[1,3,70,256]{3,2,1,0:T(8,128)(2,1)S(1)}, u32[]{:S(2)}, u32[]{:S(2)}) collective-permute-start(bf16[1,3,70,256]{3,2,1,0:T(8,128)(2,1)S(1)} %get-tuple-element.91), channel_id=1, source_target_pairs={{1,0},{2,1},{3,2},{4,3},{5,4},{6,5},{7,6},{8,7},{9,8},{10,9},{11,1... | collective-permute-start | bytes 322568 | tf_op jit(solution)/shard_map/ppermute | solution.py:15
  168.4 5.7 %collective-permute-start.7 = (bf16[1,3,70,256]{3,2,1,0:T(8,128)(2,1)S(1)}, bf16[1,3,70,256]{3,2,1,0:T(8,128)(2,1)S(1)}, u32[]{:S(2)}, u32[]{:S(2)}) collective-permute-start(bf16[1,3,70,256]{3,2,1,0:T(8,128)(2,1)S(1)} %get-tuple-element.92), channel_id=1, source_target_pairs={{0,1},{1,2},{2,3},{3,4},{4,5},{5,6},{6,7},{7,8},{8,9},{9,10},{10,1... | collective-permute-start | bytes 322568 | tf_op jit(solution)/shard_map/ppermute | solution.py:14
  440.5 2.4 copy-start.2
Sparse Core Ops, SparseCore 0:
  167.1 273.3 all-reduce.3
where the time goes:
time: 452 us; the launch traced here: 451 us
  waiting for transfers between devices  268 us (59%)
  blocking collectives  112 us (25%)
  starting transfers between devices  24.9 us (6%)
  other arithmetic  20.3 us (4%)
  between operations  14.4 us (3%)
  matrix products  5.94 us (1%)
  local copies, waits for them, and re-layouts  5.65 us (1%)
    psum x1, waiting for transfers between devices, local(): lax.psum((grad_w_in, grad_w_out, grad_b_in, grad_b_out, grad_scale, grad_...  262 us
    psum x1, blocking collectives, local(): lax.psum((grad_w_in, grad_w_out, grad_b_in, grad_b_out, grad_scale, grad_...  112 us
    ppermute x4, starting transfers between devices, extended(): after = lax.ppermute(leading, axis, down)  14 us
    ppermute x4, starting transfers between devices, extended(): before = lax.ppermute(last, axis, up)  10.9 us
  transfers between devices with their start and end apart: 9, of which 4 were waited for; matrix products, arithmetic and copies ran while one was open for 3% of the time, Pallas kernels for 0%

commit v1 on v0

--- a/solution.py
+++ b/solution.py
@@ -151,7 +151,13 @@
     grad_w_in, grad_w_out, grad_b_in, grad_b_out, grad_scale, grad_ln_gain, grad_ln_bias = (
         grad_terms
     )
-    reduced = lax.psum(
+
+    def stages_all_apply(base_x):
+        for j0 in ("lon", "lat"):
+            base_x = lax.psum(base_x, axis_name=j0)
+        return base_x
+
+    reduced = stages_all_apply(
         (
             grad_w_in,
             grad_w_out,
@@ -162,8 +168,7 @@
             grad_ln_bias,
             kernel_part,
             bias_part,
-        ),
-        ("lon", "lat"),
+        )
     )
     (
         grad_w_in,

time: 452 us -> 1370 us (3.03)
  the two profiles are of different devices: /device:TPU:1 before, /device:TPU:8 now
where the time goes in v1:
time: 1370 us
  waiting for transfers between devices  836 us (61%)
  blocking collectives  467 us (34%)
  other arithmetic  20.3 us (1%)
  starting transfers between devices  19.2 us (1%)
  between operations  14.4 us (1%)
    psum x2, waiting for transfers between devices, stages_all_apply(): base_x = lax.psum(base_x, axis_name=j0)  825 us
    psum x2, blocking collectives, stages_all_apply(): base_x = lax.psum(base_x, axis_name=j0)  467 us
  transfers between devices with their start and end apart: 10, of which 6 were waited for; matrix products, arithmetic and copies ran while one was open for 1% of the time, Pallas kernels for 0%

profile of v1, /device:TPU:8, one launch (start us, length us, event | category | flops | bytes accessed | tf_op | source)
XLA Modules:
  0.0 1367.7 jit_solution(10605783906825718013)
XLA Ops:
  7.3 0.8 fusion.147
  8.1 1.9 collective-permute-start.1
  10.0 2.4 collective-permute-start
  12.4 0.9 fusion.150
  13.4 1.0 fusion.148
  14.4 1.0 fusion.149
  15.4 0.9 constant_dynamic-update-slice_fusion.1
  17.0 2.2 collective-permute-done
  19.2 1.0 pad_maximum_fusion.2
  20.3 2.1 collective-permute-start.2
  22.4 1.3 collective-permute-start.3
  23.7 1.9 collective-permute-done.2
  25.6 4.8 collective-permute-done.3
  30.4 3.2 fusion.142
  35.7 0.9 convert_reduce_fusion.1
  36.6 1.3 convert_reduce_fusion
  38.8 0.8 fusion.102
  39.5 0.8 fusion.130
  40.3 1.4 fusion.151
  41.7 1.7 fusion.141
  43.4 2.0 collective-permute-start.4
  45.4 3.5 collective-permute-start.5
  49.0 0.7 fusion.129
  50.1 26.7 %all-reduce.2 = (f32[7,7,256]{2,1,0:T(8,128)S(1)}, f32[256]{0:T(256)S(1)}, f32[256]{0:T(256)S(1)}, f32[256]{0:T(256)S(1)}, f32[1024]{0:T(1024)S(1)}, /*index=5*/f32[256]{0:T(256)S(1)}, f32[256]{0:T(256)S(1)}) all-reduce(f32[7,7,256]{2,1,0:T(8,128)S(1)} %constant_dynamic-update-slice_fusion.2, ...), channel_id=1, replica_groups=mesh['lon'=8,'lat'=64] {'lon'}, use_global_device_ids=true, to_apply=%region_53.0 | all-reduce | flops 14848 | bytes 118784 | tf_op jit(solution)/shard_map/psum | solution.py:157
  76.8 439.9 %all-reduce = (f32[7,7,256]{2,1,0:T(8,128)S(1)}, f32[256]{0:T(256)S(1)}, f32[256]{0:T(256)S(1)}, f32[256]{0:T(256)S(1)}, f32[1024]{0:T(1024)S(1)}, /*index=5*/f32[256]{0:T(256)S(1)}, f32[256]{0:T(256)S(1)}) all-reduce(f32[7,7,256]{2,1,0:T(8,128)S(1)} %get-tuple-element.83, ...), channel_id=1, replica_groups=mesh['lon'=8,'lat'=64] {'lat'}, use_global_device_ids=true, to_apply=%region_54.0 | all-reduce | flops 14848 | bytes 118784 | tf_op jit(solution)/shard_map/psum | solution.py:157
  520.3 1.3 collective-permute-start.6
  521.6 4.6 collective-permute-start.7
  527.3 1.1 collective-permute-done.7
  528.5 3.8 fusion.55
  532.3 825.1 %all-reduce.7.cloned.1.call-done = (f32[256,1024]{1,0:T(8,128)}, f32[1024,256]{1,0:T(8,128)}) async-done(((f32[256,1024]{1,0:T(8,128)}, f32[1024,256]{1,0:T(8,128)}), (f32[256,1024]{1,0:T(8,128)}, f32[1024,256]{1,0:T(8,128)})) %all-reduce.7.cloned.1.call-update) | async-done | bytes 2097168 | tf_op jit(solution)/shard_map/psum | solution.py:157
  1357.4 2.4 broadcast_multiply_fusion.1
  1359.8 1.1 broadcast_multiply_fusion
  (73 shorter events, 8.9 us)
Async XLA Ops:
  7.2 27.0 %copy-start = (bf16[256,1024]{1,0:T(8,128)(2,1)S(1)}, bf16[256,1024]{1,0:T(8,128)(2,1)}, u32[]{:S(2)}) copy-start(bf16[256,1024]{1,0:T(8,128)(2,1)} %param.19) | copy-start | bytes 1572868
  7.2 23.1 %copy-start.1 = (bf16[1,6,64,256]{3,2,1,0:T(8,128)(2,1)S(1)}, bf16[1,6,64,256]{3,2,1,0:T(8,128)(2,1)}, u32[]{:S(2)}) copy-start(bf16[1,6,64,256]{3,2,1,0:T(8,128)(2,1)} %param.12) | copy-start | bytes 589828
  7.2 23.2 %copy-start.8 = (f32[256]{0:T(256)S(1)}, f32[256]{0:T(256)}, u32[]{:S(2)}) copy-start(f32[256]{0:T(256)} %param.16) | copy-start | bytes 3076
  7.2 511.2 %all-reduce.9.cloned.1.call-start = ((), (), s32[]{:S(2)}) async-start(), calls=%async_computation.1 | async-start | bytes 4194304 | tf_op jit(solution)/shard_map/psum | solution.py:157
  8.1 8.9 collective-permute-start.1
  10.0 9.2 collective-permute-start
  20.3 5.3 collective-permute-start.2
  22.4 8.0 collective-permute-start.3
  30.4 3.6 copy-start.5
  30.4 3.6 copy-start.7
  30.4 3.8 copy-start.4
  33.7 1.0 copy-start.9
  33.7 1.0 copy-start.10
  34.7 0.9 copy-start.3
  34.7 0.9 copy-start.6
  43.4 476.8 %collective-permute-start.4 = (bf16[1,6,3,256]{3,2,1,0:T(4,128)(2,1)S(1)}, bf16[1,6,3,256]{3,2,1,0:T(4,128)(2,1)S(1)}, u32[]{:S(2)}, u32[]{:S(2)}) collective-permute-start(bf16[1,6,3,256]{3,2,1,0:T(4,128)(2,1)S(1)} %get-tuple-element.109), channel_id=1, source_target_pairs={{0,64},{64,128},{128,192},{192,256},{256,320},{320,384},{384,448},... | collective-permute-start | bytes 27656 | tf_op jit(solution)/shard_map/ppermute | solution.py:14
  45.4 474.7 %collective-permute-start.5 = (bf16[1,6,3,256]{3,2,1,0:T(4,128)(2,1)S(1)}, bf16[1,6,3,256]{3,2,1,0:T(4,128)(2,1)S(1)}, u32[]{:S(2)}, u32[]{:S(2)}) collective-permute-start(bf16[1,6,3,256]{3,2,1,0:T(4,128)(2,1)S(1)} %get-tuple-element.108), channel_id=1, source_target_pairs={{64,0},{128,64},{192,128},{256,192},{320,256},{384,320},{448,384},... | collective-permute-start | bytes 27656 | tf_op jit(solution)/shard_map/ppermute | solution.py:15
  49.8 1307.6 %all-reduce.7.cloned.1.call-start = ((), (), s32[]{:S(2)}) async-start(), calls=%async_computation | async-start | bytes 4194304 | tf_op jit(solution)/shard_map/psum | solution.py:157
  520.3 7.0 collective-permute-start.6
  521.6 6.9 collective-permute-start.7
  1357.4 2.4 copy-start.2
Sparse Core Ops, SparseCore 0:
  49.9 96.1 all-reduce.8
  518.5 838.8 all-reduce.6
